TPU v7x, 32 devices: a whole 2x2x4 slice. The times are simulated.
32 devices in a mesh: ctx: 16 (over z, x, core), head: 2 (over y).
Axes of the slice: x: 2, y: 2, z: 4, core: 2. Of those that a mesh axis runs over, the one named last changes fastest.
Arguments:
- queries: bfloat16 [4096, 4096], P('ctx', 'head')
- keys: bfloat16 [4096, 1024], P(('ctx', 'head'))
- values: bfloat16 [4096, 1024], P(('ctx', 'head')), may hold values from -6 to 6
- selected: int32 [32, 8, 3], P('ctx', 'head'), may hold values from 0 to 6, as said below
Outputs:
- attended: bfloat16 [4096, 4096], P('ctx', 'head')
Inputs may be any that keep to these rules, and one draw needn't show every extreme that they name: selected[t, g, :] names 3 different blocks of 512 positions that lie before the block of tile t; where fewer than 3 such blocks exist, the remaining entries equal the tile's own block and name nothing more.
All inputs are finite; a program needn't handle non-finite values.
Results may differ from a plain program's by a relative error of at most 0.0041.
Values may be sent and summed in bfloat16 or wider, within the bound.
No kernel may reach another device: no remote copies, remote signals or barrier semaphores. Data moves between devices by JAX's collectives and lax.ppermute only.
A program may use at most 64 MiB of HBM per device.

v0:
```python
import math
import jax
import jax.numpy as jnp
from jax import lax
from jax.sharding import PartitionSpec as P

HD = 128
QH = 32
KVH = 8
BLK = 512
TILE = 128
floor_value = -1e30


def body(queries, keys, values, selected):
    local_rows = queries.shape[0]
    group_count = KVH // lax.axis_size("head")
    per_group = QH // KVH
    score_scale = HD ** (-0.5)
    own_keys, own_values = (
        lax.all_to_all(keys, "head", split_axis=1, concat_axis=0, tiled=True),
        lax.all_to_all(values, "head", split_axis=1, concat_axis=0, tiled=True),
    )
    query_four = queries.reshape(local_rows, group_count, per_group, HD)
    offset = lax.axis_index("ctx") * local_rows
    query_pos = offset + jnp.arange(local_rows, dtype=jnp.int32)
    query_block = query_pos // BLK
    row_select = jnp.repeat(selected, TILE, axis=0)

    def attend(running, key_rows, value_rows, first_row):
        row_count = key_rows.shape[0]
        key_pos = first_row + jnp.arange(row_count, dtype=jnp.int32)
        key_block = key_pos // BLK
        own_part = (key_block[None, :] == query_block[:, None]) & (
            key_pos[None, :] <= query_pos[:, None]
        )
        picked = jnp.any(row_select[:, :, :, None] == key_block[None, None, None, :], axis=2)
        picked = picked & (key_block[None, None, :] != query_block[:, None, None])
        allowed = jnp.transpose(picked | own_part[:, None, :], (1, 0, 2))

        def compute(current):
            running_max, totals, accumulated = current
            scores = (
                jnp.einsum(
                    "qgjd,kgd->gjqk",
                    query_four,
                    key_rows.reshape(row_count, group_count, HD),
                    preferred_element_type=jnp.float32,
                )
                * score_scale
            )
            live_mask = allowed[:, None]
            row_top = jnp.max(jnp.where(live_mask, scores, floor_value), axis=-1)
            newest = jnp.maximum(running_max, row_top)
            weights = jnp.where(live_mask, jnp.exp(scores - newest[..., None]), 0.0)
            factor = jnp.exp(running_max - newest)
            totals = totals * factor + jnp.sum(weights, axis=-1)
            product = jnp.einsum(
                "gjqk,kgd->gjqd",
                weights.astype(jnp.bfloat16),
                value_rows.reshape(row_count, group_count, HD),
                preferred_element_type=jnp.float32,
            )
            accumulated = accumulated * factor[..., None] + product
            return (newest, totals, accumulated)

        def keep_running(current):
            return current

        needed = jnp.any(allowed)
        return lax.cond(needed, compute, keep_running, running)

    start_max = jnp.full((group_count, per_group, local_rows), floor_value, jnp.float32)
    start_totals = jnp.zeros((group_count, per_group, local_rows), jnp.float32)
    start_accumulated = jnp.zeros((group_count, per_group, local_rows, HD), jnp.float32)
    key_piece = lax.all_gather(own_keys, "ctx", axis=0, tiled=True)
    value_piece = lax.all_gather(own_values, "ctx", axis=0, tiled=True)
    row_count = key_piece.shape[0]
    step_rows = math.gcd(row_count, 512)

    def loop_body(block_index, current):
        key_part = lax.dynamic_slice_in_dim(key_piece, block_index * step_rows, step_rows, 0)
        value_part = lax.dynamic_slice_in_dim(value_piece, block_index * step_rows, step_rows, 0)
        return attend(current, key_part, value_part, block_index * step_rows)

    running_max, totals, accumulated = lax.fori_loop(
        0, row_count // step_rows, loop_body, (start_max, start_totals, start_accumulated)
    )
    mixed = accumulated / totals[..., None]
    return (
        jnp.transpose(mixed, (2, 0, 1, 3))
        .reshape(local_rows, group_count * per_group * HD)
        .astype(jnp.bfloat16)
    )


def solution(mesh):
    placed = (
        P("ctx", "head"),
        P(("ctx", "head"), None),
        P(("ctx", "head"), None),
        P("ctx", "head", None),
    )
    return jax.shard_map(
        body, mesh=mesh, in_specs=placed, out_specs=P("ctx", "head"), check_vma=False
    )
```

profile of v0, /device:TPU:27, one launch (start us, length us, event | category | flops | bytes accessed | tf_op | source)
XLA Modules:
  0.0 254.5 jit_solution(11256422979810992226)
XLA Ops:
  7.8 6.7 %all_to_all.38 = bf16[128,2,512]{0,2,1:T(8,128)(2,1)S(1)} all-to-all(bf16[128,2,512]{0,2,1:T(8,128)(2,1)S(1)} %bitcast.60), channel_id=1, replica_groups=mesh['ctx'=16,'head'=2] {'head'}, dimensions={1} | all-to-all | bytes 524288 | tf_op jit(solution)/shard_map/all_to_all | solution.py:21
  16.5 6.4 %all_to_all.39 = bf16[128,2,512]{0,2,1:T(8,128)(2,1)S(1)} all-to-all(bf16[128,2,512]{0,2,1:T(8,128)(2,1)S(1)} %bitcast.61), channel_id=1, replica_groups=mesh['ctx'=16,'head'=2] {'head'}, dimensions={1} | all-to-all | bytes 524288 | tf_op jit(solution)/shard_map/all_to_all | solution.py:22
  25.8 39.4 %all-gather.3.cloned.1.call-done = bf16[4096,512]{1,0:T(8,128)(2,1)} async-done(((bf16[256,512]{1,0:T(8,128)(2,1)}), bf16[4096,512]{1,0:T(8,128)(2,1)}) %all-gather.3.cloned.1.call-update) | async-done | bytes 4194320 | tf_op jit(solution)/shard_map/all_gather | solution.py:76
  65.2 6.4 %copy.69 = bf16[4096,512]{0,1:T(8,128)(2,1)} copy(bf16[4096,512]{1,0:T(8,128)(2,1)} %all-gather.3.cloned.1.call-done) | data formatting | bytes 8388608
  71.6 44.8 %all-gather.5.cloned.1.call-done = bf16[4096,512]{1,0:T(8,128)(2,1)} async-done(((bf16[256,512]{1,0:T(8,128)(2,1)}), bf16[4096,512]{1,0:T(8,128)(2,1)}) %all-gather.5.cloned.1.call-update) | async-done | bytes 4194320 | tf_op jit(solution)/shard_map/all_gather | solution.py:77
  116.4 6.5 %copy.71 = bf16[4096,512]{0,1:T(8,128)(2,1)} copy(bf16[4096,512]{1,0:T(8,128)(2,1)} %all-gather.5.cloned.1.call-done) | data formatting | bytes 8388608
  122.9 1.6 broadcast_in_dim.69
  124.5 118.8 %while.21 = (s32[]{:T(128)}, f32[4,4,256]{2,1,0:T(4,128)S(1)}, f32[4,4,256]{2,1,0:T(4,128)S(1)}, f32[4,4,256,128]{3,2,1,0:T(8,128)}, bf16[4096,512]{0,1:T(8,128)...) while((s32[]{:T(128)}, f32[4,4,256]{2,1,0:T(4,128)S(1)}, ...), condition=%wide.region_7.8_spmd.clone.clone, body=%wide.region_0.7_spmd.clone.clone.sunk | while | flops 1103646720 | bytes 56711624 | solution.py:86
  128.2 11.1 %conditional.4 = ((f32[4,4,256]{2,1,0:T(4,128)S(1)}, f32[4,4,256]{2,1,0:T(4,128)S(1)}, f32[4,4,256,128]{3,2,1,0:T(8,128)})) conditional(s32[]{:T(128)} %convert_element_type.38, (f32[4,4,256]{2,1,0:T(4,128)S(1)}, f32[4,4,256]{2,1,0:T(4,128)S(1)}, f32[4,4,256,128]{3,2,1,0:T(8,128)}) %tuple.84, (pred[256,512]{0,1:T(8,128)(4,1)S(1)}, ...), branch_computations={%region_3.3_spmd, %region_4.6_spmd} | conditional | flops 1098915840 | bytes 54526076 | solution.py:71
  130.9 1.9 fusion.6
  132.8 1.8 fusion.10
  134.6 3.3 %multiply_add_fusion = f32[4,4,256,128]{3,2,1,0:T(8,128)S(1)} fusion(f32[4,4,256,128]{3,2,1,0:T(8,128)S(1)} %copy-done, bf16[512,4,128,1]{0,2,3,1:T(8,128)(2,1)S(1)} %bitcast.53, f32[4,512,256,4]{2,1,3,0:T(8,128)S(1)} %get-tuple-element.534, f32[4,4,256]{2,1,0:T(4,128)S(1)} %max.5, pred[4,256,512]{1,2,0:T(8,128)(4,1)S(1)} %and_or_fusion, ...), kind=kOutput, calls=%fused_computation.15 | convolution fusion | flops 546308096 | bytes 13664256 | tf_op jit(solution)/shard_map/while/body/eval_jaxpr/cond/branch_1_fun/gjqk,kgd->gjqd/dot_general | solution.py:58
  138.0 1.3 copy-done.1
  143.0 11.1 %conditional.4 = ((f32[4,4,256]{2,1,0:T(4,128)S(1)}, f32[4,4,256]{2,1,0:T(4,128)S(1)}, f32[4,4,256,128]{3,2,1,0:T(8,128)})) conditional(s32[]{:T(128)} %convert_element_type.38, (f32[4,4,256]{2,1,0:T(4,128)S(1)}, f32[4,4,256]{2,1,0:T(4,128)S(1)}, f32[4,4,256,128]{3,2,1,0:T(8,128)}) %tuple.84, (pred[256,512]{0,1:T(8,128)(4,1)S(1)}, ...), branch_computations={%region_3.3_spmd, %region_4.6_spmd} | conditional | flops 1098915840 | bytes 54526076 | solution.py:71
  145.7 1.9 fusion.6
  147.6 1.8 fusion.10
  149.5 3.3 %multiply_add_fusion = f32[4,4,256,128]{3,2,1,0:T(8,128)S(1)} fusion(f32[4,4,256,128]{3,2,1,0:T(8,128)S(1)} %copy-done, bf16[512,4,128,1]{0,2,3,1:T(8,128)(2,1)S(1)} %bitcast.53, f32[4,512,256,4]{2,1,3,0:T(8,128)S(1)} %get-tuple-element.534, f32[4,4,256]{2,1,0:T(4,128)S(1)} %max.5, pred[4,256,512]{1,2,0:T(8,128)(4,1)S(1)} %and_or_fusion, ...), kind=kOutput, calls=%fused_computation.15 | convolution fusion | flops 546308096 | bytes 13664256 | tf_op jit(solution)/shard_map/while/body/eval_jaxpr/cond/branch_1_fun/gjqk,kgd->gjqd/dot_general | solution.py:58
  152.8 1.3 copy-done.1
  157.9 11.1 %conditional.4 = ((f32[4,4,256]{2,1,0:T(4,128)S(1)}, f32[4,4,256]{2,1,0:T(4,128)S(1)}, f32[4,4,256,128]{3,2,1,0:T(8,128)})) conditional(s32[]{:T(128)} %convert_element_type.38, (f32[4,4,256]{2,1,0:T(4,128)S(1)}, f32[4,4,256]{2,1,0:T(4,128)S(1)}, f32[4,4,256,128]{3,2,1,0:T(8,128)}) %tuple.84, (pred[256,512]{0,1:T(8,128)(4,1)S(1)}, ...), branch_computations={%region_3.3_spmd, %region_4.6_spmd} | conditional | flops 1098915840 | bytes 54526076 | solution.py:71
  160.5 1.9 fusion.6
  162.5 1.8 fusion.10
  164.3 3.3 %multiply_add_fusion = f32[4,4,256,128]{3,2,1,0:T(8,128)S(1)} fusion(f32[4,4,256,128]{3,2,1,0:T(8,128)S(1)} %copy-done, bf16[512,4,128,1]{0,2,3,1:T(8,128)(2,1)S(1)} %bitcast.53, f32[4,512,256,4]{2,1,3,0:T(8,128)S(1)} %get-tuple-element.534, f32[4,4,256]{2,1,0:T(4,128)S(1)} %max.5, pred[4,256,512]{1,2,0:T(8,128)(4,1)S(1)} %and_or_fusion, ...), kind=kOutput, calls=%fused_computation.15 | convolution fusion | flops 546308096 | bytes 13664256 | tf_op jit(solution)/shard_map/while/body/eval_jaxpr/cond/branch_1_fun/gjqk,kgd->gjqd/dot_general | solution.py:58
  167.7 1.3 copy-done.1
  172.7 11.1 %conditional.4 = ((f32[4,4,256]{2,1,0:T(4,128)S(1)}, f32[4,4,256]{2,1,0:T(4,128)S(1)}, f32[4,4,256,128]{3,2,1,0:T(8,128)})) conditional(s32[]{:T(128)} %convert_element_type.38, (f32[4,4,256]{2,1,0:T(4,128)S(1)}, f32[4,4,256]{2,1,0:T(4,128)S(1)}, f32[4,4,256,128]{3,2,1,0:T(8,128)}) %tuple.84, (pred[256,512]{0,1:T(8,128)(4,1)S(1)}, ...), branch_computations={%region_3.3_spmd, %region_4.6_spmd} | conditional | flops 1098915840 | bytes 54526076 | solution.py:71
  175.4 1.9 fusion.6
  177.3 1.8 fusion.10
  179.2 3.3 %multiply_add_fusion = f32[4,4,256,128]{3,2,1,0:T(8,128)S(1)} fusion(f32[4,4,256,128]{3,2,1,0:T(8,128)S(1)} %copy-done, bf16[512,4,128,1]{0,2,3,1:T(8,128)(2,1)S(1)} %bitcast.53, f32[4,512,256,4]{2,1,3,0:T(8,128)S(1)} %get-tuple-element.534, f32[4,4,256]{2,1,0:T(4,128)S(1)} %max.5, pred[4,256,512]{1,2,0:T(8,128)(4,1)S(1)} %and_or_fusion, ...), kind=kOutput, calls=%fused_computation.15 | convolution fusion | flops 546308096 | bytes 13664256 | tf_op jit(solution)/shard_map/while/body/eval_jaxpr/cond/branch_1_fun/gjqk,kgd->gjqd/dot_general | solution.py:58
  182.5 1.3 copy-done.1
  187.6 11.1 %conditional.4 = ((f32[4,4,256]{2,1,0:T(4,128)S(1)}, f32[4,4,256]{2,1,0:T(4,128)S(1)}, f32[4,4,256,128]{3,2,1,0:T(8,128)})) conditional(s32[]{:T(128)} %convert_element_type.38, (f32[4,4,256]{2,1,0:T(4,128)S(1)}, f32[4,4,256]{2,1,0:T(4,128)S(1)}, f32[4,4,256,128]{3,2,1,0:T(8,128)}) %tuple.84, (pred[256,512]{0,1:T(8,128)(4,1)S(1)}, ...), branch_computations={%region_3.3_spmd, %region_4.6_spmd} | conditional | flops 1098915840 | bytes 54526076 | solution.py:71
  190.2 1.9 fusion.6
  192.2 1.8 fusion.10
  194.0 3.3 %multiply_add_fusion = f32[4,4,256,128]{3,2,1,0:T(8,128)S(1)} fusion(f32[4,4,256,128]{3,2,1,0:T(8,128)S(1)} %copy-done, bf16[512,4,128,1]{0,2,3,1:T(8,128)(2,1)S(1)} %bitcast.53, f32[4,512,256,4]{2,1,3,0:T(8,128)S(1)} %get-tuple-element.534, f32[4,4,256]{2,1,0:T(4,128)S(1)} %max.5, pred[4,256,512]{1,2,0:T(8,128)(4,1)S(1)} %and_or_fusion, ...), kind=kOutput, calls=%fused_computation.15 | convolution fusion | flops 546308096 | bytes 13664256 | tf_op jit(solution)/shard_map/while/body/eval_jaxpr/cond/branch_1_fun/gjqk,kgd->gjqd/dot_general | solution.py:58
  202.4 11.1 %conditional.4 = ((f32[4,4,256]{2,1,0:T(4,128)S(1)}, f32[4,4,256]{2,1,0:T(4,128)S(1)}, f32[4,4,256,128]{3,2,1,0:T(8,128)})) conditional(s32[]{:T(128)} %convert_element_type.38, (f32[4,4,256]{2,1,0:T(4,128)S(1)}, f32[4,4,256]{2,1,0:T(4,128)S(1)}, f32[4,4,256,128]{3,2,1,0:T(8,128)}) %tuple.84, (pred[256,512]{0,1:T(8,128)(4,1)S(1)}, ...), branch_computations={%region_3.3_spmd, %region_4.6_spmd} | conditional | flops 1098915840 | bytes 54526076 | solution.py:71
  205.1 1.9 fusion.6
  207.0 1.8 fusion.10
  208.9 3.3 %multiply_add_fusion = f32[4,4,256,128]{3,2,1,0:T(8,128)S(1)} fusion(f32[4,4,256,128]{3,2,1,0:T(8,128)S(1)} %copy-done, bf16[512,4,128,1]{0,2,3,1:T(8,128)(2,1)S(1)} %bitcast.53, f32[4,512,256,4]{2,1,3,0:T(8,128)S(1)} %get-tuple-element.534, f32[4,4,256]{2,1,0:T(4,128)S(1)} %max.5, pred[4,256,512]{1,2,0:T(8,128)(4,1)S(1)} %and_or_fusion, ...), kind=kOutput, calls=%fused_computation.15 | convolution fusion | flops 546308096 | bytes 13664256 | tf_op jit(solution)/shard_map/while/body/eval_jaxpr/cond/branch_1_fun/gjqk,kgd->gjqd/dot_general | solution.py:58
  217.3 11.1 %conditional.4 = ((f32[4,4,256]{2,1,0:T(4,128)S(1)}, f32[4,4,256]{2,1,0:T(4,128)S(1)}, f32[4,4,256,128]{3,2,1,0:T(8,128)})) conditional(s32[]{:T(128)} %convert_element_type.38, (f32[4,4,256]{2,1,0:T(4,128)S(1)}, f32[4,4,256]{2,1,0:T(4,128)S(1)}, f32[4,4,256,128]{3,2,1,0:T(8,128)}) %tuple.84, (pred[256,512]{0,1:T(8,128)(4,1)S(1)}, ...), branch_computations={%region_3.3_spmd, %region_4.6_spmd} | conditional | flops 1098915840 | bytes 54526076 | solution.py:71
  219.9 1.9 fusion.6
  221.9 1.8 fusion.10
  223.7 3.3 %multiply_add_fusion = f32[4,4,256,128]{3,2,1,0:T(8,128)S(1)} fusion(f32[4,4,256,128]{3,2,1,0:T(8,128)S(1)} %copy-done, bf16[512,4,128,1]{0,2,3,1:T(8,128)(2,1)S(1)} %bitcast.53, f32[4,512,256,4]{2,1,3,0:T(8,128)S(1)} %get-tuple-element.534, f32[4,4,256]{2,1,0:T(4,128)S(1)} %max.5, pred[4,256,512]{1,2,0:T(8,128)(4,1)S(1)} %and_or_fusion, ...), kind=kOutput, calls=%fused_computation.15 | convolution fusion | flops 546308096 | bytes 13664256 | tf_op jit(solution)/shard_map/while/body/eval_jaxpr/cond/branch_1_fun/gjqk,kgd->gjqd/dot_general | solution.py:58
  227.1 1.3 copy-done.1
  232.1 11.1 %conditional.4 = ((f32[4,4,256]{2,1,0:T(4,128)S(1)}, f32[4,4,256]{2,1,0:T(4,128)S(1)}, f32[4,4,256,128]{3,2,1,0:T(8,128)})) conditional(s32[]{:T(128)} %convert_element_type.38, (f32[4,4,256]{2,1,0:T(4,128)S(1)}, f32[4,4,256]{2,1,0:T(4,128)S(1)}, f32[4,4,256,128]{3,2,1,0:T(8,128)}) %tuple.84, (pred[256,512]{0,1:T(8,128)(4,1)S(1)}, ...), branch_computations={%region_3.3_spmd, %region_4.6_spmd} | conditional | flops 1098915840 | bytes 54526076 | solution.py:71
  234.8 1.9 fusion.6
  236.7 1.8 fusion.10
  238.6 3.3 %multiply_add_fusion = f32[4,4,256,128]{3,2,1,0:T(8,128)S(1)} fusion(f32[4,4,256,128]{3,2,1,0:T(8,128)S(1)} %copy-done, bf16[512,4,128,1]{0,2,3,1:T(8,128)(2,1)S(1)} %bitcast.53, f32[4,512,256,4]{2,1,3,0:T(8,128)S(1)} %get-tuple-element.534, f32[4,4,256]{2,1,0:T(4,128)S(1)} %max.5, pred[4,256,512]{1,2,0:T(8,128)(4,1)S(1)} %and_or_fusion, ...), kind=kOutput, calls=%fused_computation.15 | convolution fusion | flops 546308096 | bytes 13664256 | tf_op jit(solution)/shard_map/while/body/eval_jaxpr/cond/branch_1_fun/gjqk,kgd->gjqd/dot_general | solution.py:58
  241.9 1.3 copy-done.1
  243.3 1.9 fusion.24
  246.0 1.6 convert_element_type.27
  (170 shorter events, 55.1 us)
Async XLA Ops:
  6.5 18.1 %copy-start.2 = (bf16[256,2048]{1,0:T(8,128)(2,1)S(1)}, bf16[256,2048]{1,0:T(8,128)(2,1)}, u32[]{:S(2)}) copy-start(bf16[256,2048]{1,0:T(8,128)(2,1)} %param.8) | copy-start | bytes 3145732
  6.5 58.6 %all-gather.3.cloned.1.call-start = ((), (), s32[]{:S(2)}) async-start(), calls=%async_computation.2 | async-start | bytes 4456448 | tf_op jit(solution)/shard_map/all_gather | solution.py:76
  15.4 101.1 %all-gather.5.cloned.1.call-start = ((), (), s32[]{:S(2)}) async-start(), calls=%async_computation.3 | async-start | bytes 4456448 | tf_op jit(solution)/shard_map/all_gather | solution.py:77
  132.8 1.9 copy-start
  138.0 1.4 copy-start.1
  147.6 1.9 copy-start
  152.8 1.4 copy-start.1
  162.5 1.9 copy-start
  167.7 1.4 copy-start.1
  177.3 1.9 copy-start
  182.5 1.4 copy-start.1
  192.1 1.9 copy-start
  197.4 1.4 copy-start.1
  207.0 1.9 copy-start
  212.2 1.4 copy-start.1
  221.8 1.9 copy-start
  227.1 1.4 copy-start.1
  236.7 1.9 copy-start
  241.9 1.4 copy-start.1
Sparse Core Ops, SparseCore 0:
  15.5 49.6 all-gather.2
  67.3 49.0 all-gather.4
where the time goes:
time: 255 us; the launch traced here: 254 us
  waiting for transfers between devices  84.2 us (33%)
  local copies, waits for them, and re-layouts  56.3 us (22%)
  matrix products  41.6 us (16%)
  other arithmetic  39.5 us (15%)
  between operations  13.5 us (5%)
  blocking collectives  13.1 us (5%)
  loops' own time  6.12 us (2%)
    all_gather x1, waiting for transfers between devices, body(): value_piece = lax.all_gather(own_values, 'ctx', axis=0, tiled=True)  44.8 us
    all_gather x1, waiting for transfers between devices, body(): key_piece = lax.all_gather(own_keys, 'ctx', axis=0, tiled=True)  39.4 us
    dot_general x8, matrix products, compute(): jnp.einsum('gjqk,kgd->gjqd', weights.astype(jnp.bfloat16), value_rows.res...  26.6 us
    unnamed x9, local copies, waits for them, and re-layouts  17.2 us
    dot_general x8, matrix products, compute(): jnp.einsum('qgjd,kgd->gjqk', query_four, key_rows.reshape(row_count, grou...  15.1 us
    reduce_sum x8, other arithmetic, compute(): totals = totals * factor + jnp.sum(weights, axis=-1)  14.7 us
    cond x40, local copies, waits for them, and re-layouts  10.8 us
    dynamic_slice x8, local copies, waits for them, and re-layouts, loop_body(): lax.dynamic_slice_in_dim(value_piece, block_index * step_rows, step_rows, 0)  10.2 us
  transfers between devices with their start and end apart: 2, of which 2 were waited for; matrix products, arithmetic and copies ran while one was open for 4% of the time, Pallas kernels for 0%

commit v1 on v0

--- a/solution.py
+++ b/solution.py
@@ -10,6 +10,24 @@
 BLK = 512
 TILE = 128
 floor_value = -1e30
+
+
+def joined_along(blocks, dim):
+    blocks = jnp.moveaxis(blocks, 0, dim)
+    dims = blocks.shape
+    return blocks.reshape(*dims[:dim], dims[dim] * dims[dim + 1], *dims[dim + 2 :])
+
+
+def grow_blocks(x, axis):
+    length = lax.axis_size(axis)
+    pieces = x[None]
+    for level in range(length.bit_length() - 1):
+        bit = 1 << level
+        received = lax.ppermute(pieces, axis, [(i, i ^ bit) for i in range(length)])
+        both = jnp.stack([pieces, received])
+        upper = lax.axis_index(axis) >> level & 1
+        pieces = jnp.where(upper == 0, both, both[::-1]).reshape(-1, *x.shape)
+    return pieces
 
 
 def body(queries, keys, values, selected):
@@ -74,7 +92,7 @@
     start_totals = jnp.zeros((group_count, per_group, local_rows), jnp.float32)
     start_accumulated = jnp.zeros((group_count, per_group, local_rows, HD), jnp.float32)
     key_piece = lax.all_gather(own_keys, "ctx", axis=0, tiled=True)
-    value_piece = lax.all_gather(own_values, "ctx", axis=0, tiled=True)
+    value_piece = joined_along(grow_blocks(own_values, "ctx"), 0)
     row_count = key_piece.shape[0]
     step_rows = math.gcd(row_count, 512)
 

time: 255 us -> 325 us (1.27)
  waiting for transfers between devices: 84.2 us -> 142 us
  other arithmetic: 39.5 us -> 44.2 us
  local copies, waits for them, and re-layouts: 56.3 us -> 60.5 us
  starting transfers between devices: 0.04 us -> 3.6 us
    ppermute x0 -> x4, waiting for transfers between devices: none -> 142 us  [grow_blocks(): received = lax.ppermute(pieces, axis, [(i, i ^ bit) for i in range(length)])]
    all_gather x1 -> x0, waiting for transfers between devices: 44.8 us -> none  [body(): value_piece = lax.all_gather(own_values, 'ctx', axis=0, tiled=True)]
    all_gather x1, waiting for transfers between devices: 39.4 us -> 0.01 us  [body(): key_piece = lax.all_gather(own_keys, 'ctx', axis=0, tiled=True)]
    ppermute x0 -> x4, starting transfers between devices: none -> 3.6 us  [grow_blocks(): received = lax.ppermute(pieces, axis, [(i, i ^ bit) for i in range(length)])]
    another operation x8 -> x9, local copies, waits for them, and re-layouts: 7.71 us -> 10.8 us
    unnamed x9 -> x11, local copies, waits for them, and re-layouts: 17.2 us -> 15.9 us
  transfers between devices with their start and end apart: 2 -> 5, of which waited for: 2 -> 4; matrix products, arithmetic and copies ran while one was open for 4% -> 6% of each run, Pallas kernels for 0% -> 0%
where the time goes in v1:
time: 325 us; the launch traced here: 324 us
  waiting for transfers between devices  142 us (44%)
  local copies, waits for them, and re-layouts  60.5 us (19%)
  other arithmetic  44.2 us (14%)
  matrix products  41.6 us (13%)
  between operations  13.5 us (4%)
  blocking collectives  13.1 us (4%)
  loops' own time  5.54 us (2%)
  starting transfers between devices  3.6 us (1%)
    ppermute x4, waiting for transfers between devices, grow_blocks(): received = lax.ppermute(pieces, axis, [(i, i ^ bit) for i in range(length)])  142 us
    dot_general x8, matrix products, compute(): jnp.einsum('gjqk,kgd->gjqd', weights.astype(jnp.bfloat16), value_rows.res...  26.6 us
    unnamed x11, local copies, waits for them, and re-layouts  15.9 us
    dot_general x8, matrix products, compute(): jnp.einsum('qgjd,kgd->gjqk', query_four, key_rows.reshape(row_count, grou...  15 us
    reduce_sum x8, other arithmetic, compute(): totals = totals * factor + jnp.sum(weights, axis=-1)  14.7 us
    cond x40, local copies, waits for them, and re-layouts  10.9 us
    dynamic_slice x8, local copies, waits for them, and re-layouts, loop_body(): lax.dynamic_slice_in_dim(value_piece, block_index * step_rows, step_rows, 0)  10.2 us
    reduce_or x8, other arithmetic, attend(): needed = jnp.any(allowed)  9.28 us
  transfers between devices with their start and end apart: 5, of which 4 were waited for; matrix products, arithmetic and copies ran while one was open for 6% of the time, Pallas kernels for 0%

profile of v1, /device:TPU:27, one launch (start us, length us, event | category | flops | bytes accessed | tf_op | source)
XLA Modules:
  0.0 323.8 jit_solution(16396191385157907401)
XLA Ops:
  7.7 6.7 %all_to_all.35 = bf16[128,2,512]{0,2,1:T(8,128)(2,1)S(1)} all-to-all(bf16[128,2,512]{0,2,1:T(8,128)(2,1)S(1)} %bitcast.83), channel_id=1, replica_groups=mesh['ctx'=16,'head'=2] {'head'}, dimensions={1} | all-to-all | bytes 524288 | tf_op jit(solution)/shard_map/all_to_all | solution.py:39
  16.4 6.4 %all_to_all.36 = bf16[128,2,512]{0,2,1:T(8,128)(2,1)S(1)} all-to-all(bf16[128,2,512]{0,2,1:T(8,128)(2,1)S(1)} %bitcast.84), channel_id=1, replica_groups=mesh['ctx'=16,'head'=2] {'head'}, dimensions={1} | all-to-all | bytes 524288 | tf_op jit(solution)/shard_map/all_to_all | solution.py:40
  23.0 3.0 collective-permute-start
  27.6 12.9 %collective-permute-done.1 = bf16[2,256,512]{2,1,0:T(8,128)(2,1)S(1)} collective-permute-done((bf16[2,256,512]{2,1,0:T(8,128)(2,1)S(1)}, bf16[2,256,512]{2,1,0:T(8,128)(2,1)S(1)}, u32[]{:S(2)}, u32[]{:S(2)}) %collective-permute-start.1) | collective-permute-done | bytes 524320 | tf_op jit(solution)/shard_map/ppermute | solution.py:26
  41.1 40.1 %collective-permute-done.2 = bf16[4,256,512]{2,1,0:T(8,128)(2,1)S(1)} collective-permute-done((bf16[4,256,512]{2,1,0:T(8,128)(2,1)S(1)}, bf16[4,256,512]{2,1,0:T(8,128)(2,1)S(1)}, u32[]{:S(2)}, u32[]{:S(2)}) %collective-permute-start.2) | collective-permute-done | bytes 1048608 | tf_op jit(solution)/shard_map/ppermute | solution.py:26
  81.9 3.1 copy.91
  86.4 1.6 copy.94
  88.0 3.1 copy.92
  91.1 87.4 %collective-permute-done.3 = bf16[8,256,512]{1,0,2:T(8,128)(2,1)} collective-permute-done((bf16[8,256,512]{1,0,2:T(8,128)(2,1)}, bf16[8,256,512]{1,0,2:T(8,128)(2,1)}, u32[]{:S(2)}, u32[]{:S(2)}) %collective-permute-start.3) | collective-permute-done | bytes 2097184 | tf_op jit(solution)/shard_map/ppermute | solution.py:26
  178.5 2.6 pad_maximum_fusion
  182.4 4.2 %copy.104 = bf16[64,8,16,256]{3,1,2,0:T(8,128)(2,1)} copy(bf16[64,8,16,256]{3,2,1,0:T(8,128)(2,1)S(1)} %bitcast.72) | data formatting | bytes 8388608
  186.6 6.5 %copy.93 = bf16[4096,512]{0,1:T(8,128)(2,1)} copy(bf16[4096,512]{1,0:T(8,128)(2,1)} %all-gather.2.cloned.1.call-done) | data formatting | bytes 8388608
  193.1 1.6 broadcast_in_dim.72
  194.7 117.9 %while.21 = (s32[]{:T(128)}, f32[4,4,256]{2,1,0:T(4,128)S(1)}, f32[4,4,256]{2,1,0:T(4,128)S(1)}, f32[4,4,256,128]{3,2,1,0:T(8,128)}, bf16[4096,512]{0,1:T(8,128)...) while((s32[]{:T(128)}, f32[4,4,256]{2,1,0:T(4,128)S(1)}, ...), condition=%wide.region_7.8_spmd.clone.clone, body=%wide.region_0.7_spmd.clone.clone.sunk | while | flops 1103646720 | bytes 56711624 | solution.py:104
  198.3 11.1 %conditional.4 = ((f32[4,4,256]{2,1,0:T(4,128)S(1)}, f32[4,4,256]{2,1,0:T(4,128)S(1)}, f32[4,4,256,128]{3,2,1,0:T(8,128)})) conditional(s32[]{:T(128)} %convert_element_type.38, (f32[4,4,256]{2,1,0:T(4,128)S(1)}, f32[4,4,256]{2,1,0:T(4,128)S(1)}, f32[4,4,256,128]{3,2,1,0:T(8,128)}) %tuple.86, (pred[256,512]{0,1:T(8,128)(4,1)S(1)}, ...), branch_computations={%region_3.3_spmd, %region_4.6_spmd} | conditional | flops 1098915840 | bytes 54526076 | solution.py:89
  200.9 1.9 fusion.6
  202.9 1.8 fusion.10
  204.7 3.3 %multiply_add_fusion = f32[4,4,256,128]{3,2,1,0:T(8,128)S(1)} fusion(f32[4,4,256,128]{3,2,1,0:T(8,128)S(1)} %copy-done, bf16[512,4,128,1]{0,2,3,1:T(8,128)(2,1)S(1)} %bitcast.73, f32[4,512,256,4]{2,1,3,0:T(8,128)S(1)} %get-tuple-element.543, f32[4,4,256]{2,1,0:T(4,128)S(1)} %max.5, pred[4,256,512]{1,2,0:T(8,128)(4,1)S(1)} %and_or_fusion, ...), kind=kOutput, calls=%fused_computation.15 | convolution fusion | flops 546308096 | bytes 13664256 | tf_op jit(solution)/shard_map/while/body/eval_jaxpr/cond/branch_1_fun/gjqk,kgd->gjqd/dot_general | solution.py:76
  213.0 11.1 %conditional.4 = ((f32[4,4,256]{2,1,0:T(4,128)S(1)}, f32[4,4,256]{2,1,0:T(4,128)S(1)}, f32[4,4,256,128]{3,2,1,0:T(8,128)})) conditional(s32[]{:T(128)} %convert_element_type.38, (f32[4,4,256]{2,1,0:T(4,128)S(1)}, f32[4,4,256]{2,1,0:T(4,128)S(1)}, f32[4,4,256,128]{3,2,1,0:T(8,128)}) %tuple.86, (pred[256,512]{0,1:T(8,128)(4,1)S(1)}, ...), branch_computations={%region_3.3_spmd, %region_4.6_spmd} | conditional | flops 1098915840 | bytes 54526076 | solution.py:89
  215.7 1.9 fusion.6
  217.6 1.8 fusion.10
  219.5 3.3 %multiply_add_fusion = f32[4,4,256,128]{3,2,1,0:T(8,128)S(1)} fusion(f32[4,4,256,128]{3,2,1,0:T(8,128)S(1)} %copy-done, bf16[512,4,128,1]{0,2,3,1:T(8,128)(2,1)S(1)} %bitcast.73, f32[4,512,256,4]{2,1,3,0:T(8,128)S(1)} %get-tuple-element.543, f32[4,4,256]{2,1,0:T(4,128)S(1)} %max.5, pred[4,256,512]{1,2,0:T(8,128)(4,1)S(1)} %and_or_fusion, ...), kind=kOutput, calls=%fused_computation.15 | convolution fusion | flops 546308096 | bytes 13664256 | tf_op jit(solution)/shard_map/while/body/eval_jaxpr/cond/branch_1_fun/gjqk,kgd->gjqd/dot_general | solution.py:76
  227.8 11.1 %conditional.4 = ((f32[4,4,256]{2,1,0:T(4,128)S(1)}, f32[4,4,256]{2,1,0:T(4,128)S(1)}, f32[4,4,256,128]{3,2,1,0:T(8,128)})) conditional(s32[]{:T(128)} %convert_element_type.38, (f32[4,4,256]{2,1,0:T(4,128)S(1)}, f32[4,4,256]{2,1,0:T(4,128)S(1)}, f32[4,4,256,128]{3,2,1,0:T(8,128)}) %tuple.86, (pred[256,512]{0,1:T(8,128)(4,1)S(1)}, ...), branch_computations={%region_3.3_spmd, %region_4.6_spmd} | conditional | flops 1098915840 | bytes 54526076 | solution.py:89
  230.4 1.9 fusion.6
  232.3 1.8 fusion.10
  234.2 3.3 %multiply_add_fusion = f32[4,4,256,128]{3,2,1,0:T(8,128)S(1)} fusion(f32[4,4,256,128]{3,2,1,0:T(8,128)S(1)} %copy-done, bf16[512,4,128,1]{0,2,3,1:T(8,128)(2,1)S(1)} %bitcast.73, f32[4,512,256,4]{2,1,3,0:T(8,128)S(1)} %get-tuple-element.543, f32[4,4,256]{2,1,0:T(4,128)S(1)} %max.5, pred[4,256,512]{1,2,0:T(8,128)(4,1)S(1)} %and_or_fusion, ...), kind=kOutput, calls=%fused_computation.15 | convolution fusion | flops 546308096 | bytes 13664256 | tf_op jit(solution)/shard_map/while/body/eval_jaxpr/cond/branch_1_fun/gjqk,kgd->gjqd/dot_general | solution.py:76
  242.5 11.1 %conditional.4 = ((f32[4,4,256]{2,1,0:T(4,128)S(1)}, f32[4,4,256]{2,1,0:T(4,128)S(1)}, f32[4,4,256,128]{3,2,1,0:T(8,128)})) conditional(s32[]{:T(128)} %convert_element_type.38, (f32[4,4,256]{2,1,0:T(4,128)S(1)}, f32[4,4,256]{2,1,0:T(4,128)S(1)}, f32[4,4,256,128]{3,2,1,0:T(8,128)}) %tuple.86, (pred[256,512]{0,1:T(8,128)(4,1)S(1)}, ...), branch_computations={%region_3.3_spmd, %region_4.6_spmd} | conditional | flops 1098915840 | bytes 54526076 | solution.py:89
  245.2 1.9 fusion.6
  247.1 1.8 fusion.10
  248.9 3.3 %multiply_add_fusion = f32[4,4,256,128]{3,2,1,0:T(8,128)S(1)} fusion(f32[4,4,256,128]{3,2,1,0:T(8,128)S(1)} %copy-done, bf16[512,4,128,1]{0,2,3,1:T(8,128)(2,1)S(1)} %bitcast.73, f32[4,512,256,4]{2,1,3,0:T(8,128)S(1)} %get-tuple-element.543, f32[4,4,256]{2,1,0:T(4,128)S(1)} %max.5, pred[4,256,512]{1,2,0:T(8,128)(4,1)S(1)} %and_or_fusion, ...), kind=kOutput, calls=%fused_computation.15 | convolution fusion | flops 546308096 | bytes 13664256 | tf_op jit(solution)/shard_map/while/body/eval_jaxpr/cond/branch_1_fun/gjqk,kgd->gjqd/dot_general | solution.py:76
  257.2 11.1 %conditional.4 = ((f32[4,4,256]{2,1,0:T(4,128)S(1)}, f32[4,4,256]{2,1,0:T(4,128)S(1)}, f32[4,4,256,128]{3,2,1,0:T(8,128)})) conditional(s32[]{:T(128)} %convert_element_type.38, (f32[4,4,256]{2,1,0:T(4,128)S(1)}, f32[4,4,256]{2,1,0:T(4,128)S(1)}, f32[4,4,256,128]{3,2,1,0:T(8,128)}) %tuple.86, (pred[256,512]{0,1:T(8,128)(4,1)S(1)}, ...), branch_computations={%region_3.3_spmd, %region_4.6_spmd} | conditional | flops 1098915840 | bytes 54526076 | solution.py:89
  259.9 1.9 fusion.6
  261.8 1.8 fusion.10
  263.7 3.3 %multiply_add_fusion = f32[4,4,256,128]{3,2,1,0:T(8,128)S(1)} fusion(f32[4,4,256,128]{3,2,1,0:T(8,128)S(1)} %copy-done, bf16[512,4,128,1]{0,2,3,1:T(8,128)(2,1)S(1)} %bitcast.73, f32[4,512,256,4]{2,1,3,0:T(8,128)S(1)} %get-tuple-element.543, f32[4,4,256]{2,1,0:T(4,128)S(1)} %max.5, pred[4,256,512]{1,2,0:T(8,128)(4,1)S(1)} %and_or_fusion, ...), kind=kOutput, calls=%fused_computation.15 | convolution fusion | flops 546308096 | bytes 13664256 | tf_op jit(solution)/shard_map/while/body/eval_jaxpr/cond/branch_1_fun/gjqk,kgd->gjqd/dot_general | solution.py:76
  272.0 11.1 %conditional.4 = ((f32[4,4,256]{2,1,0:T(4,128)S(1)}, f32[4,4,256]{2,1,0:T(4,128)S(1)}, f32[4,4,256,128]{3,2,1,0:T(8,128)})) conditional(s32[]{:T(128)} %convert_element_type.38, (f32[4,4,256]{2,1,0:T(4,128)S(1)}, f32[4,4,256]{2,1,0:T(4,128)S(1)}, f32[4,4,256,128]{3,2,1,0:T(8,128)}) %tuple.86, (pred[256,512]{0,1:T(8,128)(4,1)S(1)}, ...), branch_computations={%region_3.3_spmd, %region_4.6_spmd} | conditional | flops 1098915840 | bytes 54526076 | solution.py:89
  274.6 1.9 fusion.6
  276.5 1.8 fusion.10
  278.4 3.3 %multiply_add_fusion = f32[4,4,256,128]{3,2,1,0:T(8,128)S(1)} fusion(f32[4,4,256,128]{3,2,1,0:T(8,128)S(1)} %copy-done, bf16[512,4,128,1]{0,2,3,1:T(8,128)(2,1)S(1)} %bitcast.73, f32[4,512,256,4]{2,1,3,0:T(8,128)S(1)} %get-tuple-element.543, f32[4,4,256]{2,1,0:T(4,128)S(1)} %max.5, pred[4,256,512]{1,2,0:T(8,128)(4,1)S(1)} %and_or_fusion, ...), kind=kOutput, calls=%fused_computation.15 | convolution fusion | flops 546308096 | bytes 13664256 | tf_op jit(solution)/shard_map/while/body/eval_jaxpr/cond/branch_1_fun/gjqk,kgd->gjqd/dot_general | solution.py:76
  286.7 11.1 %conditional.4 = ((f32[4,4,256]{2,1,0:T(4,128)S(1)}, f32[4,4,256]{2,1,0:T(4,128)S(1)}, f32[4,4,256,128]{3,2,1,0:T(8,128)})) conditional(s32[]{:T(128)} %convert_element_type.38, (f32[4,4,256]{2,1,0:T(4,128)S(1)}, f32[4,4,256]{2,1,0:T(4,128)S(1)}, f32[4,4,256,128]{3,2,1,0:T(8,128)}) %tuple.86, (pred[256,512]{0,1:T(8,128)(4,1)S(1)}, ...), branch_computations={%region_3.3_spmd, %region_4.6_spmd} | conditional | flops 1098915840 | bytes 54526076 | solution.py:89
  289.4 1.9 fusion.6
  291.3 1.8 fusion.10
  293.2 3.3 %multiply_add_fusion = f32[4,4,256,128]{3,2,1,0:T(8,128)S(1)} fusion(f32[4,4,256,128]{3,2,1,0:T(8,128)S(1)} %copy-done, bf16[512,4,128,1]{0,2,3,1:T(8,128)(2,1)S(1)} %bitcast.73, f32[4,512,256,4]{2,1,3,0:T(8,128)S(1)} %get-tuple-element.543, f32[4,4,256]{2,1,0:T(4,128)S(1)} %max.5, pred[4,256,512]{1,2,0:T(8,128)(4,1)S(1)} %and_or_fusion, ...), kind=kOutput, calls=%fused_computation.15 | convolution fusion | flops 546308096 | bytes 13664256 | tf_op jit(solution)/shard_map/while/body/eval_jaxpr/cond/branch_1_fun/gjqk,kgd->gjqd/dot_general | solution.py:76
  301.4 11.1 %conditional.4 = ((f32[4,4,256]{2,1,0:T(4,128)S(1)}, f32[4,4,256]{2,1,0:T(4,128)S(1)}, f32[4,4,256,128]{3,2,1,0:T(8,128)})) conditional(s32[]{:T(128)} %convert_element_type.38, (f32[4,4,256]{2,1,0:T(4,128)S(1)}, f32[4,4,256]{2,1,0:T(4,128)S(1)}, f32[4,4,256,128]{3,2,1,0:T(8,128)}) %tuple.86, (pred[256,512]{0,1:T(8,128)(4,1)S(1)}, ...), branch_computations={%region_3.3_spmd, %region_4.6_spmd} | conditional | flops 1098915840 | bytes 54526076 | solution.py:89
  304.1 1.9 fusion.6
  306.0 1.8 fusion.10
  307.9 3.3 %multiply_add_fusion = f32[4,4,256,128]{3,2,1,0:T(8,128)S(1)} fusion(f32[4,4,256,128]{3,2,1,0:T(8,128)S(1)} %copy-done, bf16[512,4,128,1]{0,2,3,1:T(8,128)(2,1)S(1)} %bitcast.73, f32[4,512,256,4]{2,1,3,0:T(8,128)S(1)} %get-tuple-element.543, f32[4,4,256]{2,1,0:T(4,128)S(1)} %max.5, pred[4,256,512]{1,2,0:T(8,128)(4,1)S(1)} %and_or_fusion, ...), kind=kOutput, calls=%fused_computation.15 | convolution fusion | flops 546308096 | bytes 13664256 | tf_op jit(solution)/shard_map/while/body/eval_jaxpr/cond/branch_1_fun/gjqk,kgd->gjqd/dot_general | solution.py:76
  312.6 1.9 fusion.24
  315.4 1.6 convert_element_type.27
  (187 shorter events, 65.7 us)
Async XLA Ops:
  6.5 180.1 %all-gather.2.cloned.1.call-start = ((), (), s32[]{:S(2)}) async-start(), calls=%async_computation.2 | async-start | bytes 4456448 | tf_op jit(solution)/shard_map/all_gather | solution.py:94
  23.0 4.2 %collective-permute-start = (bf16[1,256,512]{2,1,0:T(8,128)(2,1)S(1)}, bf16[1,256,512]{2,1,0:T(8,128)(2,1)S(1)}, u32[]{:S(2)}, u32[]{:S(2)}) collective-permute-start(bf16[1,256,512]{2,1,0:T(8,128)(2,1)S(1)} %bitcast.85), channel_id=1, source_target_pairs={{0,2},{2,0},{4,6},{6,4},{8,10},{10,8},{12,14},{14,12},{16,18},{18,... | collective-permute-start | bytes 786440 | tf_op jit(solution)/shard_map/ppermute | solution.py:26
  27.3 13.2 %collective-permute-start.1 = (bf16[2,256,512]{2,1,0:T(8,128)(2,1)S(1)}, bf16[2,256,512]{2,1,0:T(8,128)(2,1)S(1)}, u32[]{:S(2)}, u32[]{:S(2)}) collective-permute-start(bf16[2,256,512]{2,1,0:T(8,128)(2,1)S(1)} %get-tuple-element.553), channel_id=1, source_target_pairs={{0,4},{2,6},{4,0},{6,2},{8,12},{10,14},{12,8},{14,10},{16,20},{18,... | collective-permute-start | bytes 1572872 | tf_op jit(solution)/shard_map/ppermute | solution.py:26
  40.8 40.4 %collective-permute-start.2 = (bf16[4,256,512]{2,1,0:T(8,128)(2,1)S(1)}, bf16[4,256,512]{2,1,0:T(8,128)(2,1)S(1)}, u32[]{:S(2)}, u32[]{:S(2)}) collective-permute-start(bf16[4,256,512]{2,1,0:T(8,128)(2,1)S(1)} %bitcast.77), channel_id=1, source_target_pairs={{0,8},{2,10},{4,12},{6,14},{8,0},{10,2},{12,4},{14,6},{16,24},{18,... | collective-permute-start | bytes 3145736 | tf_op jit(solution)/shard_map/ppermute | solution.py:26
  81.4 3.6 %copy-start.3 = (s32[2,4,3]{1,0,2:T(2,128)S(1)}, s32[2,4,3]{1,0,2:T(2,128)}, u32[]{:S(2)}) copy-start(s32[2,4,3]{1,0,2:T(2,128)} %param.11) | copy-start | bytes 292
  81.4 3.7 %copy-start.2 = (bf16[256,2048]{1,0:T(8,128)(2,1)S(1)}, bf16[256,2048]{1,0:T(8,128)(2,1)}, u32[]{:S(2)}) copy-start(bf16[256,2048]{1,0:T(8,128)(2,1)} %param.8) | copy-start | bytes 3145732
  84.9 93.6 %collective-permute-start.3 = (bf16[8,256,512]{1,0,2:T(8,128)(2,1)}, bf16[8,256,512]{1,0,2:T(8,128)(2,1)}, u32[]{:S(2)}, u32[]{:S(2)}) collective-permute-start(bf16[8,256,512]{1,0,2:T(8,128)(2,1)} %copy.91), channel_id=1, source_target_pairs={{0,16},{2,18},{4,20},{6,22},{8,24},{10,26},{12,28},{14,30},{16,0},... | collective-permute-start | bytes 6291464 | tf_op jit(solution)/shard_map/ppermute | solution.py:26
  202.8 1.9 copy-start
  208.1 1.4 copy-start.1
  217.6 1.9 copy-start
  222.8 1.4 copy-start.1
  232.3 1.9 copy-start
  237.5 1.4 copy-start.1
  247.1 1.9 copy-start
  252.3 1.4 copy-start.1
  261.8 1.9 copy-start
  267.0 1.4 copy-start.1
  276.5 1.9 copy-start
  281.7 1.4 copy-start.1
  291.3 1.9 copy-start
  296.5 1.4 copy-start.1
  306.0 1.9 copy-start
  311.2 1.4 copy-start.1
Sparse Core Ops, SparseCore 0:
  15.4 63.6 all-gather.1
